TPU v7x, 128 devices: a whole 4x4x4 slice. The times are simulated.
128 devices in a mesh: front: 8 (over z, core), panel: 16 (over x, y).
Axes of the slice: x: 4, y: 4, z: 4, core: 2. Of those that a mesh axis runs over, the one named last changes fastest.
Arguments:
- pivot_columns: float32 [8, 8192, 1024], P('front', 'panel')
- child_rows: bfloat16 [8, 16, 16, 4, 8192], P('front', 'panel'), may hold values from -0.375 to 0.375
- slot_rows: int32 [8, 16, 16, 4], P('front', 'panel'), may hold values from -1 to 511, as said below
- parents: int32 [8], replicated, may hold values from 0 to 7, as said below
- pivot_rhs: float32 [8, 1024, 128], P('front'), may hold values from -6 to 6
- boundary_solution: float32 [8, 8192, 128], P('front', 'panel'), may hold values from -6 to 6
Outputs:
- panel_factor: float32 [8, 8192, 1024], P('front', 'panel')
- update_matrix: bfloat16 [8, 8192, 7168], P('front', 'panel')
- front_solution: float32 [8, 8192, 128], P('front', 'panel')
- child_solution: float32 [8, 16, 16, 4, 128], P('front', 'panel')
Inputs may be any that keep to these rules, and one draw needn't show every extreme that they name: parents[c] is the front of this level into which child front c's rows are added; a front may take several children or none. `slot_rows`: the live slots of each tile of 4 slots come first; the rows that one child front sends to one destination device are distinct; for each child front one destination device receives full tiles from every source device.
All inputs are finite; a program needn't handle non-finite values.
Results may differ from a plain program's by a relative error of at most 0.007.
Values may be sent and summed in bfloat16 or wider, within the bound.
A program may use at most 192 MiB of HBM per device.

v0:
```python
import jax
import jax.numpy as jnp
from jax import lax
from jax.sharding import PartitionSpec as P

K = 512
NSTEP = 2


def spread(shard, axis, root):
    mine = lax.axis_index(axis) == root
    return lax.psum(jnp.where(mine, shard, jnp.zeros_like(shard)), axis)


def outer_rows(mine, piece):
    return lax.dot_general(
        mine, piece, (((1,), (1,)), ((), ())), preferred_element_type=jnp.float32
    )


def scatter_term(slots, rows, local_ids, width):
    onehot = (slots.reshape(-1)[None, :] == local_ids[:, None]).astype(jnp.bfloat16)
    return jnp.dot(onehot, rows.reshape(-1, width), preferred_element_type=jnp.float32)


def on_device(pivot_columns, child_rows, slot_rows, parents, pivot_rhs, boundary_solution):
    highest = lax.Precision.HIGHEST
    panel_index = lax.axis_index("panel")
    front_index = lax.axis_index("front")
    piv_cols = pivot_columns[0]
    row_count = piv_cols.shape[0]
    pivots = piv_cols.shape[1]
    width = child_rows.shape[-1]
    rhs_count = pivot_rhs.shape[-1]
    local_ids = jnp.arange(row_count, dtype=jnp.int32)
    glob_rows = panel_index * row_count + local_ids
    rows_out = child_rows[0, 0]
    slots_out = slot_rows[0, 0]
    routed_rows, routed_slots = (
        lax.all_to_all(rows_out, "panel", split_axis=0, concat_axis=0, tiled=True),
        lax.all_to_all(slots_out, "panel", split_axis=0, concat_axis=0, tiled=True),
    )
    piece_rows = lax.all_gather(routed_rows[None], "front", axis=0, tiled=True)
    piece_slots = lax.all_gather(routed_slots[None], "front", axis=0, tiled=True)
    keeping = parents == front_index

    def add_rows(current):
        kept_slots = jnp.where(keeping[:, None, None], piece_slots, -1)
        return scatter_term(kept_slots, piece_rows, local_ids, width)

    def keep_same(current):
        return current

    assembled = lax.cond(
        jnp.any(keeping), add_rows, keep_same, jnp.zeros((row_count, width), jnp.float32)
    )
    work = assembled + jnp.concatenate(
        [piv_cols, jnp.zeros((row_count, width - pivots), jnp.float32)], axis=1
    )
    identity_block = jnp.eye(K, dtype=jnp.float32)

    def factor_block(values):
        lower = jnp.linalg.cholesky(values)
        return lax.linalg.triangular_solve(lower, identity_block, left_side=True, lower=True)

    def empty_block(values):
        return jnp.zeros_like(values)

    factors = []
    inverses = []
    for panel_step in range(NSTEP):
        low_edge = panel_step * K
        high_edge = low_edge + K
        root_rank = low_edge // row_count
        offset = low_edge - root_rank * row_count
        pivot_block = work[offset : offset + K, low_edge:high_edge]
        inverse = lax.cond(panel_index == root_rank, factor_block, empty_block, pivot_block)
        inverse = spread(inverse, "panel", root_rank)
        column = jnp.dot(work[:, low_edge:high_edge], inverse.T, precision=highest)
        column = jnp.where(glob_rows[:, None] >= low_edge, column, 0.0)
        packed = column.astype(jnp.bfloat16)
        factors.append(column)
        inverses.append(inverse)
        work = work - outer_rows(packed, lax.all_gather(packed, "panel", axis=0, tiled=True))
    factor_all = jnp.concatenate(factors, axis=1)
    trailing = work[:, pivots:]
    update_matrix = jnp.where(glob_rows[:, None] >= pivots, trailing, 0.0).astype(jnp.bfloat16)
    known = boundary_solution[0]
    right_side = pivot_rhs[0]

    def local_values(solved):
        extended = jnp.concatenate([solved, jnp.zeros((row_count, rhs_count), jnp.float32)], axis=0)
        begin = jnp.minimum(panel_index * row_count, pivots)
        segment = lax.dynamic_slice_in_dim(extended, begin, row_count)
        return jnp.where(glob_rows[:, None] < pivots, segment, known)

    solved = jnp.zeros((pivots, rhs_count), jnp.float32)
    contract_rows = (((0,), (0,)), ((), ()))
    for panel_step in reversed(range(NSTEP)):
        low_edge = panel_step * K
        high_edge = low_edge + K
        current = local_values(solved)
        masked = jnp.where(glob_rows[:, None] >= high_edge, factors[panel_step], 0.0)
        partial_sum = lax.dot_general(masked, current, contract_rows, precision=highest)
        carried = lax.psum(partial_sum, "panel")
        value = lax.dot_general(
            inverses[panel_step],
            right_side[low_edge:high_edge] - carried,
            contract_rows,
            precision=highest,
        )
        solved = solved.at[low_edge:high_edge].set(value)
    front_values = local_values(solved)
    slot_onehot = (routed_slots[..., None] == local_ids).astype(jnp.float32)
    piece = lax.all_gather(front_values[None], "front", axis=0, tiled=True)
    piece_count = piece.shape[0]
    weights = (jnp.arange(piece_count, dtype=jnp.int32) == parents[front_index]).astype(jnp.float32)
    chosen = jnp.einsum("n,nrh->rh", weights, piece, precision=highest)
    slot_values = jnp.einsum("psr,rh->psh", slot_onehot, chosen, precision=highest)
    child_values = lax.all_to_all(slot_values, "panel", split_axis=0, concat_axis=0, tiled=True)
    return (factor_all[None], update_matrix[None], front_values[None], child_values[None, None])


def solution(mesh):
    in_specs = (
        P("front", "panel", None),
        P("front", "panel", None, None, None),
        P("front", "panel", None, None),
        P(),
        P("front", None, None),
        P("front", "panel", None),
    )
    out_specs = (
        P("front", "panel", None),
        P("front", "panel", None),
        P("front", "panel", None),
        P("front", "panel", None, None, None),
    )
    return jax.shard_map(
        on_device, mesh=mesh, in_specs=in_specs, out_specs=out_specs, check_vma=False
    )
```

profile of v0, /device:TPU:0, one launch (start us, length us, event | category | flops | bytes accessed | tf_op | source)
XLA Modules:
  0.0 1002.9 jit_solution(4517287727802942974)
XLA Ops:
  7.2 24.1 %all_to_all.19 = bf16[16,4,8192]{2,1,0:T(4,128)(2,1)} all-to-all(bf16[16,4,8192]{2,1,0:T(4,128)(2,1)} %bitcast.145), channel_id=1, replica_groups=mesh['front'=8,'panel'=16] {'panel'}, dimensions={0} | all-to-all | bytes 2097152 | tf_op jit(solution)/shard_map/all_to_all | solution.py:40
  31.3 1.4 copy.30
  32.7 3.8 all-to-all-start
  36.7 1.3 fusion.107
  38.6 5.4 all-to-all-done
  44.0 14.0 %all-gather = s32[128,1,4]{2,1,0:T(1,128)S(1)} all-gather(s32[16,1,4]{2,1,0:T(1,128)S(1)} %all-to-all-done), channel_id=2, replica_groups=mesh['front'=8,'panel'=16] {'front'}, dimensions={0}, use_global_device_ids=true | all-gather | bytes 2304 | tf_op jit(solution)/shard_map/all_gather | solution.py:44
  58.0 22.9 %all-gather.12.cloned.1.call-done = bf16[128,4,8192]{2,1,0:T(4,128)(2,1)} async-done(((bf16[16,4,8192]{2,1,0:T(4,128)(2,1)}), bf16[128,4,8192]{2,1,0:T(4,128)(2,1)}) %all-gather.12.cloned.1.call-update) | async-done | bytes 8388624 | tf_op jit(solution)/shard_map/all_gather | solution.py:43
  80.9 24.2 %conditional.3 = (f32[512,8192]{1,0:T(8,128)}) conditional(s32[]{:T(128)} %convert_element_type.26, () %tuple.36, (pred[8]{0:T(512)(128)(4,1)S(1)}, s32[8,16,4]{2,1,0:T(8,128)S(1)}, s32[512]{0:T(512)S(1)}, bf16[8,16,4,8192]{3,2,1,0:T(4,128)(2,1)}) %tuple.137), branch_computations={%region_1.0_spmd, %region_2.3_spmd} | conditional | flops 4295229952 | bytes 41955344 | solution.py:54
  81.0 12.5 %reshape.120 = bf16[512,8192]{1,0:T(8,128)(2,1)} reshape(bf16[8,16,4,8192]{3,2,1,0:T(4,128)(2,1)} %get-tuple-element.54) | data formatting | bytes 16777216 | tf_op jit(solution)/shard_map/cond/branch_1_fun/reshape | solution.py:23
  93.6 11.5 %fusion = f32[512,8192]{1,0:T(8,128)} fusion(bf16[512,8192]{1,0:T(8,128)(2,1)} %reshape.120, s32[512]{0:T(512)S(1)} %eq.3, s32[512]{0:T(512)S(1)} %get-tuple-element.53), kind=kOutput, calls=%fused_computation | convolution fusion | flops 4295229440 | bytes 25169920 | tf_op jit(solution)/shard_map/cond/branch_1_fun/dot_general | solution.py:23
  105.0 7.0 pad_add_fusion
  112.0 5.7 copy-done
  117.8 141.4 %conditional.4 = (f32[512,512]{0,1:T(8,128)}) conditional(s32[]{:T(128)} %convert_element_type.27, () %tuple.38, (f32[512,512]{1,0:T(8,128)S(1)}, f32[512,512]{1,0:T(8,128)S(1)}) %tuple.39), branch_computations={%region_3.4_spmd, %region_4.15_spmd} | conditional | flops 1412760064 | bytes 26743068 | solution.py:77
  118.7 1.0 copy-done.2
  119.7 11.7 %cholesky.286 = f32[128,128]{1,0:T(8,128)S(1)} custom-call(f32[128,128]{1,0:T(8,128)S(1)} %cholesky.426), custom_call_target="Cholesky" | custom-call | tf_op jit(solution)/shard_map/cond/branch_1_fun/jit(cholesky)/cholesky | solution.py:63
  131.4 9.8 custom-call.27
  141.4 1.2 constant_dynamic-update-slice_fusion.3
  142.6 1.3 convolution_subtract_fusion.3
  143.9 11.7 %cholesky.305 = f32[128,128]{1,0:T(8,128)S(1)} custom-call(f32[128,128]{1,0:T(8,128)S(1)} %cholesky.430), custom_call_target="Cholesky" | custom-call | tf_op jit(solution)/shard_map/cond/branch_1_fun/jit(cholesky)/cholesky | solution.py:63
  155.6 0.7 compare_reduce_fusion.2
  157.7 10.0 %custom-call.28 = f32[1,128,128]{1,2,0:T(8,128)S(1)} custom-call(f32[1,128,128]{2,1,0:T(8,128)S(1)} %get-tuple-element.139), custom_call_target="InvertDiagBlocksLowerTriangular" | custom-call | tf_op jit(solution)/shard_map/cond/branch_1_fun/jit(cholesky)/cholesky | solution.py:63
  168.0 1.3 convolution_subtract_fusion.4
  169.3 11.7 %cholesky.326 = f32[128,128]{1,0:T(8,128)S(1)} custom-call(f32[128,128]{1,0:T(8,128)S(1)} %cholesky.435), custom_call_target="Cholesky" | custom-call | tf_op jit(solution)/shard_map/cond/branch_1_fun/jit(cholesky)/cholesky | solution.py:63
  181.1 0.6 compare_reduce_fusion.1
  182.3 9.8 custom-call.29
  192.4 1.2 convolution_subtract_fusion.5
  193.6 11.7 %cholesky.343 = f32[128,128]{1,0:T(8,128)S(1)} custom-call(f32[128,128]{1,0:T(8,128)S(1)} %convolution_subtract_fusion.5), custom_call_target="Cholesky" | custom-call | tf_op jit(solution)/shard_map/cond/branch_1_fun/jit(cholesky)/cholesky | solution.py:63
  205.3 0.6 compare_reduce_fusion
  207.2 8.0 while.6
  207.9 1.4 bitcast_dynamic-update-slice_fusion.5
  209.9 1.4 bitcast_dynamic-update-slice_fusion.5
  211.9 1.4 bitcast_dynamic-update-slice_fusion.5
  213.9 1.4 bitcast_dynamic-update-slice_fusion.5
  215.3 39.3 %custom-call.30 = f32[4,128,128]{1,2,0:T(8,128)S(1)} custom-call(f32[4,128,128]{2,1,0:T(8,128)S(1)} %get-tuple-element.77), custom_call_target="InvertDiagBlocksLowerTriangular" | custom-call | tf_op jit(solution)/shard_map/cond/branch_1_fun/triangular_solve/custom-call.3 | solution.py:64
  256.7 0.6 convolution_subtract_fusion.2
  257.8 1.3 copy.41
  259.3 2.3 broadcast_select_fusion.2
  261.7 82.1 %all-reduce.11.cloned.1.call-done = f32[512,512]{0,1:T(8,128)} async-done(((f32[512,512]{0,1:T(8,128)}), f32[512,512]{0,1:T(8,128)}) %all-reduce.11.cloned.1.call-update) | async-done | bytes 1048592 | tf_op jit(solution)/shard_map/psum | solution.py:12
  343.8 4.2 fusion.110
  348.1 77.5 %all-gather.8.cloned.1.call-done = bf16[8192,512]{0,1:T(8,128)(2,1)} async-done(((bf16[512,512]{0,1:T(8,128)(2,1)}), bf16[8192,512]{0,1:T(8,128)(2,1)}) %all-gather.8.cloned.1.call-update) | async-done | bytes 8388624 | tf_op jit(solution)/shard_map/all_gather | solution.py:84
  425.6 18.7 %convolution_subtract_fusion.12 = f32[512,8192]{1,0:T(8,128)} fusion(f32[512,8192]{1,0:T(8,128)} %copy-done, bf16[512,512]{0,1:T(8,128)(2,1)} %get-tuple-element.163, bf16[8192,512]{0,1:T(8,128)(2,1)} %all-gather.8.cloned.1.call-done), kind=kOutput, calls=%fused_computation.141 | convolution fusion | flops 4299161600 | bytes 42467328 | tf_op jit(solution)/shard_map/dot_general | solution.py:16
  444.3 1.3 slice.215
  445.6 8.3 conditional.5
  445.6 1.1 broadcast.206.clone
  453.9 1.1 broadcast_select_fusion.1
  455.1 237.6 %all-reduce.13.cloned.1.call-done = f32[512,512]{0,1:T(8,128)} async-done(((f32[512,512]{0,1:T(8,128)}), f32[512,512]{0,1:T(8,128)}) %all-reduce.13.cloned.1.call-update) | async-done | bytes 1048592 | tf_op jit(solution)/shard_map/psum | solution.py:12
  692.7 4.2 fusion.111
  697.0 1.8 fusion.69
  698.8 83.3 %all-reduce.15.cloned.1.call-done = f32[512,128]{1,0:T(8,128)} async-done(((f32[512,128]{1,0:T(8,128)}), f32[512,128]{1,0:T(8,128)}) %all-reduce.15.cloned.1.call-update) | async-done | bytes 262160 | tf_op jit(solution)/shard_map/psum | solution.py:105
  782.1 2.3 fusion.85
  784.4 1.8 fusion.71
  786.3 83.5 %all-reduce.17.cloned.1.call-done = f32[512,128]{1,0:T(8,128)} async-done(((f32[512,128]{1,0:T(8,128)}), f32[512,128]{1,0:T(8,128)}) %all-reduce.17.cloned.1.call-update) | async-done | bytes 262160 | tf_op jit(solution)/shard_map/psum | solution.py:105
  869.8 2.3 fusion.86
  872.1 0.9 fusion.82
  873.1 0.7 all-gather.10.cloned.1.call-update
  874.5 23.5 %all-gather.14.cloned.1.call-done = f32[4096,128]{1,0:T(8,128)} async-done(((f32[512,128]{1,0:T(8,128)}), f32[4096,128]{1,0:T(8,128)}) %all-gather.14.cloned.1.call-update) | async-done | bytes 2097168 | tf_op jit(solution)/shard_map/all_gather | solution.py:115
  898.0 4.4 fusion.67
  903.3 7.1 all-to-all-start.2
  910.4 1.5 maximum_bitcast_fusion
  911.9 2.9 copy.37
  914.8 3.1 all-to-all-done.2
  918.0 60.9 %all-gather.10.cloned.1.call-done = bf16[8192,512]{0,1:T(8,128)(2,1)} async-done(((bf16[512,512]{0,1:T(8,128)(2,1)}), bf16[8192,512]{0,1:T(8,128)(2,1)}) %all-gather.10.cloned.1.call-update) | async-done | bytes 8388624 | tf_op jit(solution)/shard_map/all_gather | solution.py:84
  978.8 7.1 fusion.112
  986.0 9.0 fusion.66
  (72 shorter events, 10.0 us)
Async XLA Ops:
  7.2 73.7 %all-gather.12.cloned.1.call-start = ((), (), s32[]{:S(2)}) async-start(), calls=%async_computation.9 | async-start | bytes 9437184 | tf_op jit(solution)/shard_map/all_gather | solution.py:43
  32.7 11.3 %all-to-all-start = ((s32[16,1,4]{2,1,0:T(1,128)}), s32[16,1,4]{2,1,0:T(1,128)S(1)}, u32[]{:S(2)}, u32[]{:S(2)}) async-start(s32[16,1,4]{2,1,0:T(1,128)} %copy.30), calls=%async_computation | async-start | bytes 16384 | tf_op jit(solution)/shard_map/all_to_all | solution.py:41
  36.5 307.3 %all-reduce.11.cloned.1.call-start = ((), (), s32[]{:S(2)}) async-start(), calls=%async_computation.3 | async-start | bytes 2097152 | tf_op jit(solution)/shard_map/psum | solution.py:12
  112.0 5.7 copy-start
  118.7 1.0 copy-start.2
  261.6 164.0 %all-gather.8.cloned.1.call-start = ((), (), s32[]{:S(2)}) async-start(), calls=%async_computation.4 | async-start | bytes 8912896 | tf_op jit(solution)/shard_map/all_gather | solution.py:84
  348.0 344.7 %all-reduce.13.cloned.1.call-start = ((), (), s32[]{:S(2)}) async-start(), calls=%async_computation.5 | async-start | bytes 2097152 | tf_op jit(solution)/shard_map/psum | solution.py:12
  445.6 251.4 %copy-start.4 = (f32[1,512,128]{2,1,0:T(8,128)S(1)}, f32[1,512,128]{2,1,0:T(8,128)}, u32[]{:S(2)}) copy-start(f32[1,512,128]{2,1,0:T(8,128)} %param.24) | copy-start | bytes 786436
  453.8 328.3 %copy-start.6 = (f32[1,1024,128]{2,1,0:T(8,128)S(1)}, f32[1,1024,128]{2,1,0:T(8,128)}, u32[]{:S(2)}) copy-start(f32[1,1024,128]{2,1,0:T(8,128)} %param.23) | copy-start | bytes 1572868
  453.8 419.9 %copy-start.7 = (s32[8]{0:T(128)S(1)}, s32[8]{0:T(128)}, u32[]{:S(2)}) copy-start(s32[8]{0:T(128)} %param.22) | copy-start | bytes 100
  454.9 327.2 %all-reduce.15.cloned.1.call-start = ((), (), s32[]{:S(2)}) async-start(), calls=%async_computation.7 | async-start | bytes 524288 | tf_op jit(solution)/shard_map/psum | solution.py:105
  698.8 171.0 %all-reduce.17.cloned.1.call-start = ((), (), s32[]{:S(2)}) async-start(), calls=%async_computation.8 | async-start | bytes 524288 | tf_op jit(solution)/shard_map/psum | solution.py:105
  784.4 194.4 %copy-start.1 = (bf16[512,512]{0,1:T(8,128)(2,1)S(1)}, bf16[512,512]{0,1:T(8,128)(2,1)}, u32[]{:S(2)}) copy-start(bf16[512,512]{0,1:T(8,128)(2,1)} %get-tuple-element.165) | copy-start | bytes 1572868
  786.2 111.8 %all-gather.14.cloned.1.call-start = ((), (), s32[]{:S(2)}) async-start(), calls=%async_computation.10 | async-start | bytes 2359296 | tf_op jit(solution)/shard_map/all_gather | solution.py:115
  873.0 105.8 %all-gather.10.cloned.1.call-start = ((), (), s32[]{:S(2)}) async-start(), calls=%async_computation.6 | async-start | bytes 8912896 | tf_op jit(solution)/shard_map/all_gather | solution.py:84
  903.3 14.6 %all-to-all-start.2 = ((f32[16,4,128]{2,1,0:T(4,128)}), f32[16,4,128]{2,1,0:T(4,128)S(1)}, u32[]{:S(2)}, u32[]{:S(2)}) async-start(f32[16,4,128]{2,1,0:T(4,128)} %copy.36), calls=%async_computation.2 | async-start | bytes 65536 | tf_op jit(solution)/shard_map/all_to_all | solution.py:120
Sparse Core Ops, SparseCore 0:
  31.4 49.3 all-gather.11
  261.7 82.0 all-reduce.10
  348.1 77.4 all-gather.7
  455.1 237.5 all-reduce.12
  698.9 83.2 all-reduce.14
  786.3 83.3 all-reduce.16
  873.2 24.8 all-gather.13
  900.1 78.6 all-gather.9
where the time goes:
time: 1010 us; the launch traced here: 1000 us
  waiting for transfers between devices  681 us (67%)
  other arithmetic  142 us (14%)
  matrix products  67.1 us (7%)
  blocking collectives  38.1 us (4%)
  local copies, waits for them, and re-layouts  37.7 us (4%)
  between operations  15.5 us (2%)
  starting transfers between devices  11.3 us (1%)
  loops' own time  10.5 us (1%)
    psum x2, waiting for transfers between devices, spread(): return lax.psum(jnp.where(mine, shard, jnp.zeros_like(shard)), axis)  320 us
    psum x2, waiting for transfers between devices, on_device(): carried = lax.psum(partial_sum, 'panel')  167 us
    all_gather x2, waiting for transfers between devices, on_device(): lax.all_gather(packed, 'panel', axis=0, tiled=True)  138 us
    another operation x14, other arithmetic, factor_block(): lower = jnp.linalg.cholesky(values)  78.6 us
    another operation x5, other arithmetic, factor_block(): lax.linalg.triangular_solve(lower, identity_block, left_side=True, lower=...  40 us
    dot_general x2, matrix products, outer_rows(): lax.dot_general(mine, piece, (((1,), (1,)), ((), ())), preferred_element_...  25.8 us
    all_to_all x1, blocking collectives, on_device(): lax.all_to_all(rows_out, 'panel', split_axis=0, concat_axis=0, tiled=True)  24.1 us
    all_gather x1, waiting for transfers between devices, on_device(): piece = lax.all_gather(front_values[None], 'front', axis=0, tiled=True)  23.5 us
  transfers between devices with their start and end apart: 10, of which 10 were waited for; matrix products, arithmetic and copies ran while one was open for 1% of the time, Pallas kernels for 0%

commit v1 on v0

--- a/solution.py
+++ b/solution.py
@@ -102,7 +102,8 @@
         current = local_values(solved)
         masked = jnp.where(glob_rows[:, None] >= high_edge, factors[panel_step], 0.0)
         partial_sum = lax.dot_general(masked, current, contract_rows, precision=highest)
-        carried = lax.psum(partial_sum, "panel")
+        blocks = lax.all_gather(partial_sum, "panel")
+        carried = jnp.sum(blocks, axis=0)
         value = lax.dot_general(
             inverses[panel_step],
             right_side[low_edge:high_edge] - carried,

time: 1010 us -> 956 us (0.947)
  waiting for transfers between devices: 681 us -> 614 us
  other arithmetic: 142 us -> 153 us
    psum x2 -> x0, waiting for transfers between devices: 167 us -> none  [on_device(): carried = lax.psum(partial_sum, 'panel')]
    all_gather x0 -> x2, waiting for transfers between devices: none -> 101 us  [on_device(): blocks = lax.all_gather(partial_sum, 'panel')]
  transfers between devices with their start and end apart: 10 -> 10, of which waited for: 10 -> 9; matrix products, arithmetic and copies ran while one was open for 1% -> 4% of each run, Pallas kernels for 0% -> 0%
where the time goes in v1:
time: 956 us; the launch traced here: 950 us
  waiting for transfers between devices  614 us (64%)
  other arithmetic  153 us (16%)
  matrix products  72.4 us (8%)
  blocking collectives  38.1 us (4%)
  local copies, waits for them, and re-layouts  37.7 us (4%)
  between operations  15.5 us (2%)
  starting transfers between devices  11.3 us (1%)
    psum x2, waiting for transfers between devices, spread(): return lax.psum(jnp.where(mine, shard, jnp.zeros_like(shard)), axis)  322 us
    all_gather x2, waiting for transfers between devices, on_device(): lax.all_gather(packed, 'panel', axis=0, tiled=True)  146 us
    all_gather x2, waiting for transfers between devices, on_device(): blocks = lax.all_gather(partial_sum, 'panel')  101 us
    another operation x14, other arithmetic, factor_block(): lower = jnp.linalg.cholesky(values)  78.6 us
    another operation x5, other arithmetic, factor_block(): lax.linalg.triangular_solve(lower, identity_block, left_side=True, lower=...  40 us
    dot_general x2, matrix products, outer_rows(): lax.dot_general(mine, piece, (((1,), (1,)), ((), ())), preferred_element_...  30.3 us
    all_to_all x1, blocking collectives, on_device(): lax.all_to_all(rows_out, 'panel', split_axis=0, concat_axis=0, tiled=True)  24.1 us
    all_gather x1, waiting for transfers between devices, on_device(): piece_rows = lax.all_gather(routed_rows[None], 'front', axis=0, tiled=True)  22.9 us
  transfers between devices with their start and end apart: 10, of which 9 were waited for; matrix products, arithmetic and copies ran while one was open for 4% of the time, Pallas kernels for 0%

profile of v1, /device:TPU:0, one launch (start us, length us, event | category | flops | bytes accessed | tf_op | source)
XLA Modules:
  0.0 949.5 jit_solution(5342520572423745340)
XLA Ops:
  7.2 24.1 %all_to_all.19 = bf16[16,4,8192]{2,1,0:T(4,128)(2,1)} all-to-all(bf16[16,4,8192]{2,1,0:T(4,128)(2,1)} %bitcast.149), channel_id=1, replica_groups=mesh['front'=8,'panel'=16] {'panel'}, dimensions={0} | all-to-all | bytes 2097152 | tf_op jit(solution)/shard_map/all_to_all | solution.py:40
  31.3 1.4 copy.30
  32.7 3.8 all-to-all-start
  36.7 1.3 fusion.107
  38.6 5.4 all-to-all-done
  44.0 14.0 %all-gather = s32[128,1,4]{2,1,0:T(1,128)S(1)} all-gather(s32[16,1,4]{2,1,0:T(1,128)S(1)} %all-to-all-done), channel_id=2, replica_groups=mesh['front'=8,'panel'=16] {'front'}, dimensions={0}, use_global_device_ids=true | all-gather | bytes 2304 | tf_op jit(solution)/shard_map/all_gather | solution.py:44
  58.0 22.9 %all-gather.16.cloned.1.call-done = bf16[128,4,8192]{2,1,0:T(4,128)(2,1)} async-done(((bf16[16,4,8192]{2,1,0:T(4,128)(2,1)}), bf16[128,4,8192]{2,1,0:T(4,128)(2,1)}) %all-gather.16.cloned.1.call-update) | async-done | bytes 8388624 | tf_op jit(solution)/shard_map/all_gather | solution.py:43
  80.9 24.2 %conditional.3 = (f32[512,8192]{1,0:T(8,128)}) conditional(s32[]{:T(128)} %convert_element_type.26, () %tuple.36, (pred[8]{0:T(512)(128)(4,1)S(1)}, s32[8,16,4]{2,1,0:T(8,128)S(1)}, s32[512]{0:T(512)S(1)}, bf16[8,16,4,8192]{3,2,1,0:T(4,128)(2,1)}) %tuple.137), branch_computations={%region_1.0_spmd, %region_2.3_spmd} | conditional | flops 4295229952 | bytes 41955344 | solution.py:54
  81.0 12.5 %reshape.120 = bf16[512,8192]{1,0:T(8,128)(2,1)} reshape(bf16[8,16,4,8192]{3,2,1,0:T(4,128)(2,1)} %get-tuple-element.54) | data formatting | bytes 16777216 | tf_op jit(solution)/shard_map/cond/branch_1_fun/reshape | solution.py:23
  93.6 11.5 %fusion = f32[512,8192]{1,0:T(8,128)} fusion(bf16[512,8192]{1,0:T(8,128)(2,1)} %reshape.120, s32[512]{0:T(512)S(1)} %eq.3, s32[512]{0:T(512)S(1)} %get-tuple-element.53), kind=kOutput, calls=%fused_computation | convolution fusion | flops 4295229440 | bytes 25169920 | tf_op jit(solution)/shard_map/cond/branch_1_fun/dot_general | solution.py:23
  105.0 7.0 pad_add_fusion
  112.0 5.7 copy-done
  117.8 141.4 %conditional.4 = (f32[512,512]{0,1:T(8,128)}) conditional(s32[]{:T(128)} %convert_element_type.27, () %tuple.38, (f32[512,512]{1,0:T(8,128)S(1)}, f32[512,512]{1,0:T(8,128)S(1)}) %tuple.39), branch_computations={%region_3.4_spmd, %region_4.15_spmd} | conditional | flops 1412760064 | bytes 26743068 | solution.py:77
  118.7 1.0 copy-done.3
  119.7 11.7 %cholesky.286 = f32[128,128]{1,0:T(8,128)S(1)} custom-call(f32[128,128]{1,0:T(8,128)S(1)} %cholesky.426), custom_call_target="Cholesky" | custom-call | tf_op jit(solution)/shard_map/cond/branch_1_fun/jit(cholesky)/cholesky | solution.py:63
  131.4 9.8 %custom-call.27 = f32[1,128,128]{1,2,0:T(8,128)S(1)} custom-call(f32[1,128,128]{2,1,0:T(8,128)S(1)} %get-tuple-element.142), custom_call_target="InvertDiagBlocksLowerTriangular" | custom-call | tf_op jit(solution)/shard_map/cond/branch_1_fun/jit(cholesky)/cholesky | solution.py:63
  141.4 1.2 constant_dynamic-update-slice_fusion.3
  142.6 1.3 convolution_subtract_fusion.3
  143.9 11.7 %cholesky.305 = f32[128,128]{1,0:T(8,128)S(1)} custom-call(f32[128,128]{1,0:T(8,128)S(1)} %cholesky.430), custom_call_target="Cholesky" | custom-call | tf_op jit(solution)/shard_map/cond/branch_1_fun/jit(cholesky)/cholesky | solution.py:63
  155.6 0.7 compare_reduce_fusion.2
  157.7 10.0 %custom-call.28 = f32[1,128,128]{1,2,0:T(8,128)S(1)} custom-call(f32[1,128,128]{2,1,0:T(8,128)S(1)} %get-tuple-element.139), custom_call_target="InvertDiagBlocksLowerTriangular" | custom-call | tf_op jit(solution)/shard_map/cond/branch_1_fun/jit(cholesky)/cholesky | solution.py:63
  168.0 1.3 convolution_subtract_fusion.4
  169.3 11.7 %cholesky.326 = f32[128,128]{1,0:T(8,128)S(1)} custom-call(f32[128,128]{1,0:T(8,128)S(1)} %cholesky.435), custom_call_target="Cholesky" | custom-call | tf_op jit(solution)/shard_map/cond/branch_1_fun/jit(cholesky)/cholesky | solution.py:63
  181.1 0.6 compare_reduce_fusion.1
  182.3 9.8 %custom-call.29 = f32[1,128,128]{1,2,0:T(8,128)S(1)} custom-call(f32[1,128,128]{2,1,0:T(8,128)S(1)} %get-tuple-element.136), custom_call_target="InvertDiagBlocksLowerTriangular" | custom-call | tf_op jit(solution)/shard_map/cond/branch_1_fun/jit(cholesky)/cholesky | solution.py:63
  192.4 1.2 convolution_subtract_fusion.5
  193.6 11.7 %cholesky.343 = f32[128,128]{1,0:T(8,128)S(1)} custom-call(f32[128,128]{1,0:T(8,128)S(1)} %convolution_subtract_fusion.5), custom_call_target="Cholesky" | custom-call | tf_op jit(solution)/shard_map/cond/branch_1_fun/jit(cholesky)/cholesky | solution.py:63
  205.3 0.6 compare_reduce_fusion
  207.2 8.0 while.6
  207.9 1.4 bitcast_dynamic-update-slice_fusion.5
  209.9 1.4 bitcast_dynamic-update-slice_fusion.5
  211.9 1.4 bitcast_dynamic-update-slice_fusion.5
  213.9 1.4 bitcast_dynamic-update-slice_fusion.5
  215.3 39.3 %custom-call.30 = f32[4,128,128]{1,2,0:T(8,128)S(1)} custom-call(f32[4,128,128]{2,1,0:T(8,128)S(1)} %get-tuple-element.77), custom_call_target="InvertDiagBlocksLowerTriangular" | custom-call | tf_op jit(solution)/shard_map/cond/branch_1_fun/triangular_solve/custom-call.3 | solution.py:64
  257.8 1.3 copy.41
  259.3 2.3 broadcast_select_fusion.2
  261.7 82.1 %all-reduce.9.cloned.1.call-done = f32[512,512]{0,1:T(8,128)} async-done(((f32[512,512]{0,1:T(8,128)}), f32[512,512]{0,1:T(8,128)}) %all-reduce.9.cloned.1.call-update) | async-done | bytes 1048592 | tf_op jit(solution)/shard_map/psum | solution.py:12
  343.8 4.2 fusion.110
  348.1 77.5 %all-gather.12.cloned.1.call-done = bf16[8192,512]{0,1:T(8,128)(2,1)} async-done(((bf16[512,512]{0,1:T(8,128)(2,1)}), bf16[8192,512]{0,1:T(8,128)(2,1)}) %all-gather.12.cloned.1.call-update) | async-done | bytes 8388624 | tf_op jit(solution)/shard_map/all_gather | solution.py:84
  425.6 18.7 %convolution_subtract_fusion.12 = f32[512,8192]{1,0:T(8,128)} fusion(f32[512,8192]{1,0:T(8,128)} %copy-done, bf16[512,512]{0,1:T(8,128)(2,1)} %get-tuple-element.163, bf16[8192,512]{0,1:T(8,128)(2,1)} %all-gather.12.cloned.1.call-done), kind=kOutput, calls=%fused_computation.141 | convolution fusion | flops 4299161600 | bytes 42467328 | tf_op jit(solution)/shard_map/dot_general | solution.py:16
  444.3 1.3 slice.215
  445.6 5.8 conditional.5
  445.6 1.1 broadcast.206.clone
  451.4 1.1 broadcast_select_fusion.1
  452.6 240.2 %all-reduce.11.cloned.1.call-done = f32[512,512]{0,1:T(8,128)} async-done(((f32[512,512]{0,1:T(8,128)}), f32[512,512]{0,1:T(8,128)}) %all-reduce.11.cloned.1.call-update) | async-done | bytes 1048592 | tf_op jit(solution)/shard_map/psum | solution.py:12
  692.9 4.3 fusion.111
  697.2 1.8 fusion.69
  699.1 50.7 %all-gather.18.cloned.1.call-done = f32[8192,128]{1,0:T(8,128)} async-done(((f32[512,128]{1,0:T(8,128)}), f32[8192,128]{1,0:T(8,128)}) %all-gather.18.cloned.1.call-update) | async-done | bytes 4194320 | tf_op jit(solution)/shard_map/all_gather | solution.py:105
  749.8 3.1 reduce_sum.18
  752.9 2.0 fusion.85
  754.9 2.7 fusion.71
  757.7 0.7 all-gather.14.cloned.1.call-update
  758.7 50.2 %all-gather.20.cloned.1.call-done = f32[8192,128]{1,0:T(8,128)} async-done(((f32[512,128]{1,0:T(8,128)}), f32[8192,128]{1,0:T(8,128)}) %all-gather.20.cloned.1.call-update) | async-done | bytes 4194320 | tf_op jit(solution)/shard_map/all_gather | solution.py:105
  808.9 2.4 reduce_sum.19
  811.3 2.3 fusion.86
  813.6 1.9 fusion.82
  816.2 1.5 maximum_bitcast_fusion
  817.6 2.9 copy.37
  820.5 68.5 %all-gather.14.cloned.1.call-done = bf16[8192,512]{0,1:T(8,128)(2,1)} async-done(((bf16[512,512]{0,1:T(8,128)(2,1)}), bf16[8192,512]{0,1:T(8,128)(2,1)}) %all-gather.14.cloned.1.call-update) | async-done | bytes 8388624 | tf_op jit(solution)/shard_map/all_gather | solution.py:84
  889.0 11.7 %fusion.112 = f32[512,8192]{1,0:T(8,128)} fusion(bf16[512,512]{0,1:T(8,128)(2,1)S(1)} %copy-done.1, bf16[8192,512]{0,1:T(8,128)(2,1)} %all-gather.14.cloned.1.call-done), kind=kOutput, calls=%fused_computation.204 | convolution fusion | flops 4294967296 | bytes 25690112 | tf_op jit(solution)/shard_map/dot_general | solution.py:16
  900.7 15.5 %all-gather.22.cloned.1.call-done = f32[4096,128]{1,0:T(8,128)} async-done(((f32[512,128]{1,0:T(8,128)}), f32[4096,128]{1,0:T(8,128)}) %all-gather.22.cloned.1.call-update) | async-done | bytes 2097168 | tf_op jit(solution)/shard_map/all_gather | solution.py:116
  916.1 4.4 fusion.67
  921.4 6.8 all-to-all-start.2
  928.3 13.3 %fusion.66 = bf16[1,512,7168]{2,1,0:T(8,128)(2,1)} fusion(f32[512,8192]{1,0:T(8,128)} %fusion.112, f32[512,8192]{1,0:T(8,128)} %convolution_subtract_fusion.12, pred[512]{0:T(512)(128)(4,1)S(1)} %fusion.95), kind=kLoop, calls=%fused_computation.142 | loop fusion | flops 11010048 | bytes 36700672 | tf_op jit(solution)/shard_map/broadcast_in_dim | solution.py:122
  (74 shorter events, 10.9 us)
Async XLA Ops:
  7.2 73.7 %all-gather.16.cloned.1.call-start = ((), (), s32[]{:S(2)}) async-start(), calls=%async_computation.7 | async-start | bytes 9437184 | tf_op jit(solution)/shard_map/all_gather | solution.py:43
  32.7 11.3 %all-to-all-start = ((s32[16,1,4]{2,1,0:T(1,128)}), s32[16,1,4]{2,1,0:T(1,128)S(1)}, u32[]{:S(2)}, u32[]{:S(2)}) async-start(s32[16,1,4]{2,1,0:T(1,128)} %copy.30), calls=%async_computation | async-start | bytes 16384 | tf_op jit(solution)/shard_map/all_to_all | solution.py:41
  36.5 307.3 %all-reduce.9.cloned.1.call-start = ((), (), s32[]{:S(2)}) async-start(), calls=%async_computation.3 | async-start | bytes 2097152 | tf_op jit(solution)/shard_map/psum | solution.py:12
  112.0 5.7 copy-start
  118.7 1.0 copy-start.3
  261.6 164.0 %all-gather.12.cloned.1.call-start = ((), (), s32[]{:S(2)}) async-start(), calls=%async_computation.4 | async-start | bytes 8912896 | tf_op jit(solution)/shard_map/all_gather | solution.py:84
  348.0 344.9 %all-reduce.11.cloned.1.call-start = ((), (), s32[]{:S(2)}) async-start(), calls=%async_computation.5 | async-start | bytes 2097152 | tf_op jit(solution)/shard_map/psum | solution.py:12
  445.6 251.6 %copy-start.5 = (f32[1,512,128]{2,1,0:T(8,128)S(1)}, f32[1,512,128]{2,1,0:T(8,128)}, u32[]{:S(2)}) copy-start(f32[1,512,128]{2,1,0:T(8,128)} %param.24) | copy-start | bytes 786436
  452.5 297.3 %all-gather.18.cloned.1.call-start = ((), (), s32[]{:S(2)}) async-start(), calls=%async_computation.8 | async-start | bytes 4456448 | tf_op jit(solution)/shard_map/all_gather | solution.py:105
  692.9 60.0 %copy-start.2 = (f32[512,512]{0,1:T(8,128)S(1)}, f32[512,512]{0,1:T(8,128)}, u32[]{:S(2)}) copy-start(f32[512,512]{0,1:T(8,128)} %all-reduce.11.cloned.1.call-done) | copy-start | bytes 3145732
  699.0 116.5 %copy-start.7 = (s32[8]{0:T(128)S(1)}, s32[8]{0:T(128)}, u32[]{:S(2)}) copy-start(s32[8]{0:T(128)} %param.22) | copy-start | bytes 100
  699.0 109.9 %all-gather.20.cloned.1.call-start = ((), (), s32[]{:S(2)}) async-start(), calls=%async_computation.9 | async-start | bytes 4456448 | tf_op jit(solution)/shard_map/all_gather | solution.py:105
  757.6 131.4 %copy-start.1 = (bf16[512,512]{0,1:T(8,128)(2,1)S(1)}, bf16[512,512]{0,1:T(8,128)(2,1)}, u32[]{:S(2)}) copy-start(bf16[512,512]{0,1:T(8,128)(2,1)} %get-tuple-element.165) | copy-start | bytes 1572868
  757.7 131.3 %all-gather.14.cloned.1.call-start = ((), (), s32[]{:S(2)}) async-start(), calls=%async_computation.6 | async-start | bytes 8912896 | tf_op jit(solution)/shard_map/all_gather | solution.py:84
  758.4 157.7 %all-gather.22.cloned.1.call-start = ((), (), s32[]{:S(2)}) async-start(), calls=%async_computation.10 | async-start | bytes 2359296 | tf_op jit(solution)/shard_map/all_gather | solution.py:116
  921.4 20.2 %all-to-all-start.2 = ((f32[16,4,128]{2,1,0:T(4,128)}), f32[16,4,128]{2,1,0:T(4,128)S(1)}, u32[]{:S(2)}, u32[]{:S(2)}) async-start(f32[16,4,128]{2,1,0:T(4,128)} %copy.36), calls=%async_computation.2 | async-start | bytes 65536 | tf_op jit(solution)/shard_map/all_to_all | solution.py:121
Sparse Core Ops, SparseCore 0:
  31.4 49.3 all-gather.15
  261.7 82.0 all-reduce.8
  348.1 77.4 all-gather.11
  452.6 240.2 all-reduce.10
  699.1 50.6 all-gather.17
  757.8 51.0 all-gather.19
  811.0 77.9 all-gather.13
  891.3 24.7 all-gather.21
